TPU v7x, 128 devices: a whole 4x4x4 slice. The times are simulated.
128 devices in a mesh: filt: 8 (over z, x_hi), space: 16 (over x_lo, y, core).
Axes of the slice: x: 4 (x_hi: 2, x_lo: 2; x = x_hi * 2 + x_lo), y: 4, z: 4, core: 2. Of those that a mesh axis runs over, the one named last changes fastest.
Arguments:
- inputs: bfloat16 [16, 256, 2048], P('space', 'filt'), may hold values from -6 to 6
- weight: bfloat16 [3, 3, 3, 256, 256], P(None, None, None, 'filt'), may hold values from -0.078125 to 0.078125
- bias: bfloat16 [256], P('filt'), may hold values from -4 to 4
- cotangent: bfloat16 [16, 256, 2048], P('space', 'filt'), may hold values from -6 to 6
Outputs:
- output: float32 [16, 256, 2048], P('space', 'filt')
- grad_inputs: float32 [16, 256, 2048], P('space', 'filt')
- grad_weight: float32 [3, 3, 3, 256, 256], P(None, None, None, 'filt')
- grad_bias: float32 [256], P('filt')
All inputs are finite; a program needn't handle non-finite values.
Results may differ from a plain program's by a relative error of at most 0.0003.
Values may be sent and summed in bfloat16 or wider, within the bound.
No kernel may reach another device: no remote copies, remote signals or barrier semaphores. Data moves between devices by JAX's collectives and lax.ppermute only.
A program may use at most 64 MiB of HBM per device.

v0:
```python
import jax
import jax.numpy as jnp
from jax import lax
from jax.sharding import PartitionSpec as P

ROWS = 32
WIDE = 64


def extended(cells, sides, width):
    for axis, dim in sides:
        count = lax.axis_size(axis)
        ends = count - 1
        head = lax.slice_in_dim(cells, 0, width, axis=dim)
        tail = lax.slice_in_dim(cells, cells.shape[dim] - width, cells.shape[dim], axis=dim)
        cells = jnp.concatenate(
            [
                lax.ppermute(tail, axis, [(i, (i + 1) % count) for i in range(ends)]),
                cells,
                lax.ppermute(head, axis, [((i + 1) % count, i) for i in range(ends)]),
            ],
            axis=dim,
        )
    return cells


def convolve_padded(padded, kernel):
    volume = padded.reshape(padded.shape[0], padded.shape[1], ROWS, WIDE)
    result = lax.conv_general_dilated(
        volume[None],
        kernel,
        (1, 1, 1),
        [(0, 0), (1, 1), (1, 1)],
        dimension_numbers=("NDCHW", "DHWIO", "NDCHW"),
        preferred_element_type=jnp.float32,
    )
    return result[0].reshape(result.shape[1], result.shape[2], ROWS * WIDE)


def body(inputs, weight, bias, cotangent):
    planes = inputs.shape[0]
    own_channels = inputs.shape[1]
    padded_in = extended(inputs, (("space", 0),), 1)
    partial_out = convolve_padded(padded_in, weight)
    summed = lax.psum_scatter(partial_out, "filt", scatter_dimension=1, tiled=True)
    output = summed + bias.astype(jnp.float32)[None, :, None]
    all_grad = lax.all_gather(cotangent, "filt", axis=1, tiled=True)
    padded_grad = extended(all_grad, (("space", 0),), 1)
    back_kernel = jnp.swapaxes(jnp.flip(weight, (0, 1, 2)), 3, 4)
    grad_inputs = convolve_padded(padded_grad, back_kernel)
    shaped_in = padded_in.reshape(planes + 2, own_channels, ROWS, WIDE)
    framed = jnp.pad(shaped_in, ((0, 0), (0, 0), (1, 1), (1, 1)))
    grad_vol = all_grad.reshape(planes, all_grad.shape[1], ROWS, WIDE)
    terms = []
    for depth_off in range(3):
        for row_off in range(3):
            for col_off in range(3):
                window = framed[
                    depth_off : depth_off + planes,
                    :,
                    row_off : row_off + ROWS,
                    col_off : col_off + WIDE,
                ]
                terms.append(
                    lax.dot_general(
                        window,
                        grad_vol,
                        (((0, 2, 3), (0, 2, 3)), ((), ())),
                        preferred_element_type=jnp.float32,
                    )
                )
    kernel_part = jnp.stack(terms).reshape(3, 3, 3, own_channels, grad_vol.shape[1])
    bias_part = jnp.sum(cotangent.astype(jnp.float32), axis=(0, 2))
    kernel_total, bias_total = lax.psum((kernel_part, bias_part), "space")
    factor = 1.0 / jnp.sqrt(jnp.float32(planes * lax.axis_size("space") * ROWS * WIDE))
    return (output, grad_inputs, kernel_total * factor, bias_total * factor)


def solution(mesh):
    placed = (
        P("space", "filt", None),
        P(None, None, None, "filt", None),
        P("filt"),
        P("space", "filt", None),
    )
    return jax.shard_map(
        body,
        mesh=mesh,
        in_specs=placed,
        out_specs=(
            P("space", "filt", None),
            P("space", "filt", None),
            P(None, None, None, "filt", None),
            P("filt"),
        ),
        check_vma=False,
    )
```

profile of v0, /device:TPU:1, one launch (start us, length us, event | category | flops | bytes accessed | tf_op | source)
XLA Modules:
  0.0 326.3 jit_solution(3926293909356311096)
XLA Ops:
  7.2 4.7 %collective-permute-start = (bf16[1,32,2048]{2,1,0:T(8,128)(2,1)}, bf16[1,32,2048]{2,1,0:T(8,128)(2,1)S(1)}, u32[]{:S(2)}, u32[]{:S(2)}) collective-permute-start(bf16[1,32,2048]{2,1,0:T(8,128)(2,1)} %param.4), channel_id=1, source_target_pairs={{0,1},{1,2},{2,3},{3,4},{4,5},{5,6},{6,7},{7,8},{8,9},{9,10},{10,1... | collective-permute-start | bytes 393224 | tf_op jit(solution)/shard_map/ppermute | solution.py:18
  12.0 1.9 collective-permute-start.1
  14.2 1.0 constant_dynamic-update-slice_fusion.1
  15.2 3.4 %collective-permute-done.1 = bf16[1,32,2048]{2,1,0:T(8,128)(2,1)S(1)} collective-permute-done((bf16[1,32,2048]{2,1,0:T(8,128)(2,1)}, bf16[1,32,2048]{2,1,0:T(8,128)(2,1)S(1)}, u32[]{:S(2)}, u32[]{:S(2)}) %collective-permute-start.1) | collective-permute-done | bytes 131104 | tf_op jit(solution)/shard_map/ppermute | solution.py:20
  18.5 0.8 reshape.169
  19.3 0.8 reshape.214
  20.5 2.1 copy.50
  22.6 3.0 pad.5.clone
  25.6 3.9 %copy.35 = bf16[3,32,32,1,8,9]{1,4,5,2,0,3:T(8,128)(2,1)} copy(bf16[3,32,32,1,8,9]{2,1,5,4,0,3:T(8,128)(2,1)} %bitcast.299) | data formatting | bytes 884736 | tf_op jit(solution)/shard_map/conv_general_dilated | solution.py:29
  29.5 1.1 slice.109
  30.7 3.9 %fusion.17 = f32[1,32,8,9,256]{4,2,3,1,0:T(8,128)S(1)} fusion(bf16[3,3,3,32,256]{4,3,2,1,0:T(8,128)(2,1)S(1)} %copy-done, bf16[3,32,32,1,7,2]{1,4,5,2,0,3:T(8,128)(2,1)S(1)} %slice.109, bf16[3,32,32,1,8,9]{1,4,5,2,0,3:T(8,128)(2,1)} %copy.35, pred[8,9]{0,1:T(8,128)(4,1)S(1)} %copy-done.9), kind=kOutput, calls=%fused_computation.19 | convolution fusion | flops 1000194048 | bytes 3330120 | tf_op jit(solution)/shard_map/conv_general_dilated | solution.py:29
  34.6 0.8 copy.36
  35.6 2.5 copy.37
  38.1 6.1 %copy.38 = f32[1,256,2048]{2,0,1:T(1,128)} copy(f32[1,256,2048]{1,2,0:T(8,128)} %bitcast.298) | data formatting | bytes 4194304 | tf_op jit(solution)/shard_map/reshape;squeeze | solution.py:37
  44.5 14.0 %all-gather.2.cloned.1.call-done = bf16[1,256,2048]{2,1,0:T(8,128)(2,1)} async-done(((bf16[1,32,2048]{2,1,0:T(8,128)(2,1)}), bf16[1,256,2048]{2,1,0:T(8,128)(2,1)}) %all-gather.2.cloned.1.call-update) | async-done | bytes 1048592 | tf_op jit(solution)/shard_map/all_gather | solution.py:47
  58.5 1.5 copy.39
  70.9 0.9 copy-done.2
  71.9 0.6 dynamic-slice
  73.1 4.2 %collective-permute-start.3 = (bf16[1,256,2048]{1,2,0:T(8,128)(2,1)S(1)}, bf16[1,256,2048]{1,2,0:T(8,128)(2,1)S(1)}, u32[]{:S(2)}, u32[]{:S(2)}) collective-permute-start(bf16[1,256,2048]{1,2,0:T(8,128)(2,1)S(1)} %copy.39), channel_id=1, source_target_pairs={{1,0},{2,1},{3,2},{4,3},{5,4},{6,5},{7,6},{8,7},{9,8},{10,9},{11,1... | collective-permute-start | bytes 3145736 | tf_op jit(solution)/shard_map/ppermute | solution.py:20
  77.3 3.0 collective-permute-start.2
  80.5 45.1 %psum.15 = f32[32]{0:T(128)S(1)} all-reduce(f32[32]{0:T(128)S(1)} %convert_reduce_fusion), channel_id=1, replica_groups=mesh['filt'=8,'space'=16] {'space'}, use_global_device_ids=true, to_apply=%region_3.4 | all-reduce | flops 32 | bytes 256 | tf_op jit(solution)/shard_map/psum | solution.py:74
  126.1 52.8 %all-reduce.7.cloned.1.call-done = f32[1,256,2048]{2,0,1:T(1,128)} async-done(((f32[1,256,2048]{2,0,1:T(1,128)}), f32[1,256,2048]{2,0,1:T(1,128)}) %all-reduce.7.cloned.1.call-update) | async-done | bytes 2097168
  178.9 1.2 dynamic-slice_add_fusion
  180.1 0.8 copy.49
  180.8 119.8 %all-reduce.5.cloned.1.call-done = f32[3,3,3,32,256]{4,3,2,1,0:T(8,128)} async-done(((f32[3,3,3,32,256]{4,3,2,1,0:T(8,128)}), f32[3,3,3,32,256]{4,3,2,1,0:T(8,128)}) %all-reduce.5.cloned.1.call-update) | async-done | bytes 884752 | tf_op jit(solution)/shard_map/psum | solution.py:74
  300.6 2.2 broadcast_multiply_fusion
  302.8 1.6 pad_maximum_fusion
  304.4 1.8 copy.51
  306.6 2.1 copy.44
  308.9 8.9 %fusion.20 = f32[1,32,8,9,32]{4,2,3,1,0:T(8,128)S(1)} fusion(bf16[3,3,3,32,256]{4,3,2,1,0:T(8,128)(2,1)S(1)} %copy-done, bf16[3,256,32,1,7,2]{1,4,5,2,0,3:T(8,128)(2,1)S(1)} %slice.111, bf16[3,256,32,1,8,9]{1,4,5,2,0,3:T(8,128)(2,1)S(1)} %copy.44, pred[8,9]{0,1:T(8,128)(4,1)S(1)} %copy-done.10), kind=kOutput, calls=%fused_computation.20 | convolution fusion | flops 1011032064 | bytes 4964424 | tf_op jit(solution)/shard_map/conv_general_dilated | solution.py:29
  318.1 0.8 copy.46
  318.8 0.9 reshape_squeeze.7
  (68 shorter events, 13.5 us)
Async XLA Ops:
  7.2 23.5 %copy-start = (bf16[3,3,3,32,256]{4,3,2,1,0:T(8,128)(2,1)S(1)}, bf16[3,3,3,32,256]{4,3,2,1,0:T(8,128)(2,1)}, u32[]{:S(2)}) copy-start(bf16[3,3,3,32,256]{4,3,2,1,0:T(8,128)(2,1)} %param.5) | copy-start | bytes 1327108
  7.2 51.4 %all-gather.2.cloned.1.call-start = ((), (), s32[]{:S(2)}) async-start(), calls=%async_computation | async-start | bytes 1179648 | tf_op jit(solution)/shard_map/all_gather | solution.py:47
  7.2 7.0 %collective-permute-start = (bf16[1,32,2048]{2,1,0:T(8,128)(2,1)}, bf16[1,32,2048]{2,1,0:T(8,128)(2,1)S(1)}, u32[]{:S(2)}, u32[]{:S(2)}) collective-permute-start(bf16[1,32,2048]{2,1,0:T(8,128)(2,1)} %param.4), channel_id=1, source_target_pairs={{0,1},{1,2},{2,3},{3,4},{4,5},{5,6},{6,7},{7,8},{8,9},{9,10},{10,1... | collective-permute-start | bytes 393224 | tf_op jit(solution)/shard_map/ppermute | solution.py:18
  12.0 166.9 %all-reduce.7.cloned.1.call-start = ((), (), s32[]{:S(2)}) async-start(), calls=%async_computation.2 | async-start | bytes 4194304
  12.0 6.5 %collective-permute-start.1 = (bf16[1,32,2048]{2,1,0:T(8,128)(2,1)}, bf16[1,32,2048]{2,1,0:T(8,128)(2,1)S(1)}, u32[]{:S(2)}, u32[]{:S(2)}) collective-permute-start(bf16[1,32,2048]{2,1,0:T(8,128)(2,1)} %param.4), channel_id=1, source_target_pairs={{1,0},{2,1},{3,2},{4,3},{5,4},{6,5},{7,6},{8,7},{9,8},{10,9},{11,1... | collective-permute-start | bytes 393224 | tf_op jit(solution)/shard_map/ppermute | solution.py:20
  14.2 4.3 %copy-start.4 = (bf16[1,32,2048]{2,1,0:T(8,128)(2,1)}, bf16[1,32,2048]{2,1,0:T(8,128)(2,1)S(1)}, u32[]{:S(2)}) copy-start(bf16[1,32,2048]{2,1,0:T(8,128)(2,1)S(1)} %collective-permute-done) | copy-start | bytes 393220
  25.6 5.1 %copy-start.9 = (pred[8,9]{0,1:T(8,128)(4,1)S(1)}, pred[8,9]{0,1:T(8,128)(4,1)}, u32[]{:S(2)}) copy-start(pred[8,9]{0,1:T(8,128)(4,1)} %constant.20) | copy-start | bytes 220
  44.3 256.4 %all-reduce.5.cloned.1.call-start = ((), (), s32[]{:S(2)}) async-start(), calls=%async_computation.1 | async-start | bytes 1769472 | tf_op jit(solution)/shard_map/psum | solution.py:74
  60.4 1.2 copy-start.1
  60.5 1.2 copy-start.5
  64.1 1.2 copy-start.3
  70.1 1.7 copy-start.7
  70.2 1.7 copy-start.8
  70.2 10.2 %copy-start.6 = (bf16[1,32,2048]{2,1,0:T(8,128)(2,1)S(1)}, bf16[1,32,2048]{2,1,0:T(8,128)(2,1)}, u32[]{:S(2)}) copy-start(bf16[1,32,2048]{2,1,0:T(8,128)(2,1)} %param.7) | copy-start | bytes 393220
  70.9 0.9 copy-start.2
  73.1 229.7 %collective-permute-start.3 = (bf16[1,256,2048]{1,2,0:T(8,128)(2,1)S(1)}, bf16[1,256,2048]{1,2,0:T(8,128)(2,1)S(1)}, u32[]{:S(2)}, u32[]{:S(2)}) collective-permute-start(bf16[1,256,2048]{1,2,0:T(8,128)(2,1)S(1)} %copy.39), channel_id=1, source_target_pairs={{1,0},{2,1},{3,2},{4,3},{5,4},{6,5},{7,6},{8,7},{9,8},{10,9},{11,1... | collective-permute-start | bytes 3145736 | tf_op jit(solution)/shard_map/ppermute | solution.py:20
  77.3 225.5 %collective-permute-start.2 = (bf16[1,256,2048]{1,2,0:T(8,128)(2,1)S(1)}, bf16[1,256,2048]{1,2,0:T(8,128)(2,1)}, u32[]{:S(2)}, u32[]{:S(2)}) collective-permute-start(bf16[1,256,2048]{1,2,0:T(8,128)(2,1)S(1)} %copy.39), channel_id=1, source_target_pairs={{0,1},{1,2},{2,3},{3,4},{4,5},{5,6},{6,7},{7,8},{8,9},{9,10},{10,1... | collective-permute-start | bytes 3145736 | tf_op jit(solution)/shard_map/ppermute | solution.py:18
  306.6 2.3 copy-start.10
Sparse Core Ops, SparseCore 0:
  12.1 46.3 all-gather.1
  61.1 117.7 all-reduce.6
  181.9 118.6 all-reduce.4
where the time goes:
time: 327 us; the launch traced here: 326 us
  waiting for transfers between devices  190 us (58%)
  blocking collectives  45.1 us (14%)
  local copies, waits for them, and re-layouts  33 us (10%)
  matrix products  23.5 us (7%)
  between operations  14.8 us (5%)
  starting transfers between devices  14.1 us (4%)
  other arithmetic  5.6 us (2%)
    psum x1, waiting for transfers between devices, body(): kernel_total, bias_total = lax.psum((kernel_part, bias_part), 'space')  120 us
    unnamed x4, waiting for transfers between devices  52.8 us
    psum x1, blocking collectives, body(): kernel_total, bias_total = lax.psum((kernel_part, bias_part), 'space')  45.1 us
    all_gather x1, waiting for transfers between devices, body(): all_grad = lax.all_gather(cotangent, 'filt', axis=1, tiled=True)  14 us
    conv_general_dilated x2, matrix products, convolve_padded(): lax.conv_general_dilated(volume[None], kernel, (1, 1, 1), [(0, 0), (1, 1)...  12.8 us
    conv_general_dilated x10, local copies, waits for them, and re-layouts, convolve_padded(): lax.conv_general_dilated(volume[None], kernel, (1, 1, 1), [(0, 0), (1, 1)...  11.9 us
    dot_general x27, matrix products, body(): lax.dot_general(window, grad_vol, (((0, 2, 3), (0, 2, 3)), ((), ())), pre...  10.7 us
    ppermute x2, starting transfers between devices, extended(): lax.ppermute(tail, axis, [(i, (i + 1) % count) for i in range(ends)])  7.73 us
  transfers between devices with their start and end apart: 7, of which 5 were waited for; matrix products, arithmetic and copies ran while one was open for 14% of the time, Pallas kernels for 0%

commit v1 on v0

--- a/solution.py
+++ b/solution.py
@@ -44,7 +44,8 @@
     partial_out = convolve_padded(padded_in, weight)
     summed = lax.psum_scatter(partial_out, "filt", scatter_dimension=1, tiled=True)
     output = summed + bias.astype(jnp.float32)[None, :, None]
-    all_grad = lax.all_gather(cotangent, "filt", axis=1, tiled=True)
+    sent = jnp.stack([cotangent] * lax.axis_size("filt"))
+    all_grad = jnp.concatenate(lax.all_to_all(sent, "filt", 0, 0), axis=1)
     padded_grad = extended(all_grad, (("space", 0),), 1)
     back_kernel = jnp.swapaxes(jnp.flip(weight, (0, 1, 2)), 3, 4)
     grad_inputs = convolve_padded(padded_grad, back_kernel)

time: 327 us -> 307 us (0.939)
  waiting for transfers between devices: 190 us -> 161 us
  local copies, waits for them, and re-layouts: 33 us -> 54.5 us
  blocking collectives: 45.1 us -> 26.3 us
  starting transfers between devices: 14.1 us -> 20.1 us
    psum x1, waiting for transfers between devices: 120 us -> 70.9 us  [body(): kernel_total, bias_total = lax.psum((kernel_part, bias_part), 'space')]
    unnamed x4 -> x3, waiting for transfers between devices: 52.8 us -> 86.8 us
    psum x1, blocking collectives: 45.1 us -> 26.3 us  [body(): kernel_total, bias_total = lax.psum((kernel_part, bias_part), 'space')]
    all_gather x1 -> x0, waiting for transfers between devices: 14 us -> none  [body(): all_grad = lax.all_gather(cotangent, 'filt', axis=1, tiled=True)]
    another operation x0 -> x6, local copies, waits for them, and re-layouts: none -> 10.9 us
    all_to_all x0 -> x1, starting transfers between devices: none -> 8.31 us  [body(): all_grad = jnp.concatenate(lax.all_to_all(sent, 'filt', 0, 0), axis=1)]
    concatenate x1 -> x4, local copies, waits for them, and re-layouts: 0.01 us -> 6.31 us  [extended(): jnp.concatenate([lax.ppermute(tail, axis, [(i, (i + 1) % count) for i in...]
    ppermute x0 -> x2, local copies, waits for them, and re-layouts: none -> 4.6 us  [the longest x1 2.34 us: extended(): lax.ppermute(tail, axis, [(i, (i + 1) % count) for i in range(ends)])]
  transfers between devices with their start and end apart: 7 -> 7, of which waited for: 5 -> 3; matrix products, arithmetic and copies ran while one was open for 14% -> 20% of each run, Pallas kernels for 0% -> 0%
where the time goes in v1:
time: 307 us; the launch traced here: 306 us
  waiting for transfers between devices  161 us (52%)
  local copies, waits for them, and re-layouts  54.5 us (18%)
  blocking collectives  26.3 us (9%)
  matrix products  23.4 us (8%)
  starting transfers between devices  20.1 us (7%)
  between operations  15 us (5%)
  other arithmetic  5.6 us (2%)
    unnamed x3, waiting for transfers between devices  86.8 us
    psum x1, waiting for transfers between devices, body(): kernel_total, bias_total = lax.psum((kernel_part, bias_part), 'space')  70.9 us
    psum x1, blocking collectives, body(): kernel_total, bias_total = lax.psum((kernel_part, bias_part), 'space')  26.3 us
    conv_general_dilated x2, matrix products, convolve_padded(): lax.conv_general_dilated(volume[None], kernel, (1, 1, 1), [(0, 0), (1, 1)...  12.9 us
    conv_general_dilated x10, local copies, waits for them, and re-layouts, convolve_padded(): lax.conv_general_dilated(volume[None], kernel, (1, 1, 1), [(0, 0), (1, 1)...  12.6 us
    dot_general x27, matrix products, body(): lax.dot_general(window, grad_vol, (((0, 2, 3), (0, 2, 3)), ((), ())), pre...  10.5 us
    another operation x5, local copies, waits for them, and re-layouts  8.81 us
    all_to_all x1, starting transfers between devices, body(): all_grad = jnp.concatenate(lax.all_to_all(sent, 'filt', 0, 0), axis=1)  8.31 us
  transfers between devices with their start and end apart: 7, of which 3 were waited for; matrix products, arithmetic and copies ran while one was open for 20% of the time, Pallas kernels for 0%

profile of v1, /device:TPU:1, one launch (start us, length us, event | category | flops | bytes accessed | tf_op | source)
XLA Modules:
  0.0 306.2 jit_solution(5146965281777670745)
XLA Ops:
  7.2 2.1 stack.95
  9.3 8.3 %all-to-all-start = ((bf16[8,1,32,2048]{3,2,1,0:T(8,128)(2,1)}), bf16[8,1,32,2048]{3,2,1,0:T(8,128)(2,1)S(1)}, u32[]{:S(2)}, u32[]{:S(2)}) async-start(bf16[8,1,32,2048]{3,2,1,0:T(8,128)(2,1)} %stack.95), calls=%async_computation | async-start | bytes 2097152 | tf_op jit(solution)/shard_map/all_to_all | solution.py:48
  17.6 4.0 %collective-permute-start = (bf16[1,32,2048]{2,1,0:T(8,128)(2,1)S(1)}, bf16[1,32,2048]{2,1,0:T(8,128)(2,1)S(1)}, u32[]{:S(2)}, u32[]{:S(2)}) collective-permute-start(bf16[1,32,2048]{2,1,0:T(8,128)(2,1)S(1)} %copy-done.6), channel_id=1, source_target_pairs={{0,1},{1,2},{2,3},{3,4},{4,5},{5,6},{6,7},{7,8},{8,9},{9,10},{10,1... | collective-permute-start | bytes 393224 | tf_op jit(solution)/shard_map/ppermute | solution.py:18
  21.7 1.9 collective-permute-start.1
  23.6 1.0 reshape.186
  24.6 3.7 %collective-permute-done.1 = bf16[1,32,2048]{2,1,0:T(8,128)(2,1)S(1)} collective-permute-done((bf16[1,32,2048]{2,1,0:T(8,128)(2,1)S(1)}, bf16[1,32,2048]{2,1,0:T(8,128)(2,1)S(1)}, u32[]{:S(2)}, u32[]{:S(2)}) %collective-permute-start.1) | collective-permute-done | bytes 131104 | tf_op jit(solution)/shard_map/ppermute | solution.py:20
  29.1 1.7 reshape.215
  31.1 3.1 %copy.141 = bf16[3,32,32,1,64]{2,1,4,0,3:T(8,128)(2,1)} copy(bf16[3,32,32,1,64]{4,2,1,0,3:T(8,128)(2,1)} %reshape.215) | data formatting | bytes 786432
  34.2 3.0 pad.5.clone
  37.1 3.9 %copy.97 = bf16[3,32,32,1,8,9]{1,4,5,2,0,3:T(8,128)(2,1)} copy(bf16[3,32,32,1,8,9]{2,1,5,4,0,3:T(8,128)(2,1)} %bitcast.274) | data formatting | bytes 884736 | tf_op jit(solution)/shard_map/conv_general_dilated | solution.py:29
  41.1 1.9 slice.109
  43.9 1.0 reshape.195
  44.8 3.2 %reshape.173 = bf16[256,32,64]{2,1,0:T(8,128)(2,1)} reshape(bf16[8,1,32,2048]{3,2,1,0:T(8,128)(2,1)S(1)} %all-to-all-done) | data formatting | bytes 2097152 | tf_op jit(solution)/shard_map/reshape.6
  48.0 2.8 copy.110
  62.6 4.0 %fusion.17 = f32[1,32,8,9,256]{4,2,3,1,0:T(8,128)S(1)} fusion(bf16[3,3,3,32,256]{4,3,2,1,0:T(8,128)(2,1)S(1)} %copy-done, bf16[3,32,32,1,7,2]{1,4,5,2,0,3:T(8,128)(2,1)} %slice.109, bf16[3,32,32,1,8,9]{1,4,5,2,0,3:T(8,128)(2,1)} %copy.97, pred[8,9]{0,1:T(8,128)(4,1)S(1)} %copy-done.10), kind=kOutput, calls=%fused_computation.19 | convolution fusion | flops 1000194048 | bytes 3330120 | tf_op jit(solution)/shard_map/conv_general_dilated | solution.py:29
  67.4 1.9 collective-permute-start.3
  69.3 3.6 %collective-permute-start.2 = (bf16[1,256,2048]{2,1,0:T(8,128)(2,1)S(1)}, bf16[1,256,2048]{2,1,0:T(8,128)(2,1)}, u32[]{:S(2)}, u32[]{:S(2)}) collective-permute-start(bf16[1,256,2048]{2,1,0:T(8,128)(2,1)S(1)} %bitcast.271), channel_id=1, source_target_pairs={{0,1},{1,2},{2,3},{3,4},{4,5},{5,6},{6,7},{7,8},{8,9},{9,10},{10,1... | collective-permute-start | bytes 3145736 | tf_op jit(solution)/shard_map/ppermute | solution.py:18
  73.2 2.5 copy.99
  75.7 6.2 %copy.100 = f32[1,256,2048]{2,0,1:T(1,128)} copy(f32[1,256,2048]{1,2,0:T(8,128)} %bitcast.273) | data formatting | bytes 4194304 | tf_op jit(solution)/shard_map/reshape;squeeze | solution.py:37
  83.4 26.3 %psum.15 = f32[32]{0:T(128)S(1)} all-reduce(f32[32]{0:T(128)S(1)} %convert_reduce_fusion), channel_id=1, replica_groups=mesh['filt'=8,'space'=16] {'space'}, use_global_device_ids=true, to_apply=%region_3.4 | all-reduce | flops 32 | bytes 256 | tf_op jit(solution)/shard_map/psum | solution.py:75
  110.1 3.2 %concatenate.15 = bf16[1,1,256,32,64]{4,3,2,1,0:T(8,128)(2,1)} reshape(bf16[8,1,32,2048]{3,2,1,0:T(8,128)(2,1)S(1)} %all-to-all-done) | data formatting | bytes 2097152 | tf_op jit(solution)/shard_map/concatenate | solution.py:16
  113.3 2.8 copy.103
  116.1 70.9 %all-reduce.5.cloned.1.call-done = f32[3,3,3,32,256]{4,3,2,1,0:T(8,128)} async-done(((f32[3,3,3,32,256]{4,3,2,1,0:T(8,128)}), f32[3,3,3,32,256]{4,3,2,1,0:T(8,128)}) %all-reduce.5.cloned.1.call-update) | async-done | bytes 884752 | tf_op jit(solution)/shard_map/psum | solution.py:75
  187.0 2.2 broadcast_multiply_fusion
  189.2 2.3 copy.102
  191.5 2.3 copy.101
  193.8 1.6 maximum_bitcast_fusion
  195.4 1.8 copy.142
  197.5 2.1 copy.106
  199.8 8.9 %fusion.20 = f32[1,32,8,9,32]{4,2,3,1,0:T(8,128)S(1)} fusion(bf16[3,3,3,32,256]{4,3,2,1,0:T(8,128)(2,1)S(1)} %copy-done, bf16[3,256,32,1,7,2]{1,4,5,2,0,3:T(8,128)(2,1)S(1)} %slice.111, bf16[3,256,32,1,8,9]{1,4,5,2,0,3:T(8,128)(2,1)S(1)} %copy.106, pred[8,9]{0,1:T(8,128)(4,1)S(1)} %copy-done.10), kind=kOutput, calls=%fused_computation.20 | convolution fusion | flops 1011032064 | bytes 4964424 | tf_op jit(solution)/shard_map/conv_general_dilated | solution.py:29
  210.7 86.7 %all-reduce.7.cloned.1.call-done = f32[1,256,2048]{2,0,1:T(1,128)} async-done(((f32[1,256,2048]{2,0,1:T(1,128)}), f32[1,256,2048]{2,0,1:T(1,128)}) %all-reduce.7.cloned.1.call-update) | async-done | bytes 2097168
  297.4 1.2 dynamic-slice_add_fusion
  (76 shorter events, 19.4 us)
Async XLA Ops:
  7.2 55.4 %copy-start = (bf16[3,3,3,32,256]{4,3,2,1,0:T(8,128)(2,1)S(1)}, bf16[3,3,3,32,256]{4,3,2,1,0:T(8,128)(2,1)}, u32[]{:S(2)}) copy-start(bf16[3,3,3,32,256]{4,3,2,1,0:T(8,128)(2,1)} %param.5) | copy-start | bytes 1327108
  7.2 10.4 %copy-start.6 = (bf16[1,32,2048]{2,1,0:T(8,128)(2,1)S(1)}, bf16[1,32,2048]{2,1,0:T(8,128)(2,1)}, u32[]{:S(2)}) copy-start(bf16[1,32,2048]{2,1,0:T(8,128)(2,1)} %param.4) | copy-start | bytes 393220
  9.3 35.6 %all-to-all-start = ((bf16[8,1,32,2048]{3,2,1,0:T(8,128)(2,1)}), bf16[8,1,32,2048]{3,2,1,0:T(8,128)(2,1)S(1)}, u32[]{:S(2)}, u32[]{:S(2)}) async-start(bf16[8,1,32,2048]{3,2,1,0:T(8,128)(2,1)} %stack.95), calls=%async_computation | async-start | bytes 2097152 | tf_op jit(solution)/shard_map/all_to_all | solution.py:48
  17.6 169.4 %all-reduce.5.cloned.1.call-start = ((), (), s32[]{:S(2)}) async-start(), calls=%async_computation.1 | async-start | bytes 1769472 | tf_op jit(solution)/shard_map/psum | solution.py:75
  17.6 6.9 %collective-permute-start = (bf16[1,32,2048]{2,1,0:T(8,128)(2,1)S(1)}, bf16[1,32,2048]{2,1,0:T(8,128)(2,1)S(1)}, u32[]{:S(2)}, u32[]{:S(2)}) collective-permute-start(bf16[1,32,2048]{2,1,0:T(8,128)(2,1)S(1)} %copy-done.6), channel_id=1, source_target_pairs={{0,1},{1,2},{2,3},{3,4},{4,5},{5,6},{6,7},{7,8},{8,9},{9,10},{10,1... | collective-permute-start | bytes 393224 | tf_op jit(solution)/shard_map/ppermute | solution.py:18
  21.7 6.6 %collective-permute-start.1 = (bf16[1,32,2048]{2,1,0:T(8,128)(2,1)S(1)}, bf16[1,32,2048]{2,1,0:T(8,128)(2,1)S(1)}, u32[]{:S(2)}, u32[]{:S(2)}) collective-permute-start(bf16[1,32,2048]{2,1,0:T(8,128)(2,1)S(1)} %copy-done.6), channel_id=1, source_target_pairs={{1,0},{2,1},{3,2},{4,3},{5,4},{6,5},{7,6},{8,7},{9,8},{10,9},{11,1... | collective-permute-start | bytes 393224 | tf_op jit(solution)/shard_map/ppermute | solution.py:20
  51.2 1.2 copy-start.4
  54.7 1.2 copy-start.2
  58.3 1.2 copy-start.3
  60.6 1.9 copy-start.10
  61.4 0.9 copy-start.5
  62.3 235.1 %all-reduce.7.cloned.1.call-start = ((), (), s32[]{:S(2)}) async-start(), calls=%async_computation.2 | async-start | bytes 4194304
  67.4 121.8 %collective-permute-start.3 = (bf16[1,256,2048]{2,1,0:T(8,128)(2,1)S(1)}, bf16[1,256,2048]{2,1,0:T(8,128)(2,1)}, u32[]{:S(2)}, u32[]{:S(2)}) collective-permute-start(bf16[1,256,2048]{2,1,0:T(8,128)(2,1)S(1)} %bitcast.270), channel_id=1, source_target_pairs={{1,0},{2,1},{3,2},{4,3},{5,4},{6,5},{7,6},{8,7},{9,8},{10,9},{11,1... | collective-permute-start | bytes 3145736 | tf_op jit(solution)/shard_map/ppermute | solution.py:20
  69.3 122.2 %collective-permute-start.2 = (bf16[1,256,2048]{2,1,0:T(8,128)(2,1)S(1)}, bf16[1,256,2048]{2,1,0:T(8,128)(2,1)}, u32[]{:S(2)}, u32[]{:S(2)}) collective-permute-start(bf16[1,256,2048]{2,1,0:T(8,128)(2,1)S(1)} %bitcast.271), channel_id=1, source_target_pairs={{0,1},{1,2},{2,3},{3,4},{4,5},{5,6},{6,7},{7,8},{8,9},{9,10},{10,1... | collective-permute-start | bytes 3145736 | tf_op jit(solution)/shard_map/ppermute | solution.py:18
  75.7 6.2 %copy-start.8 = (bf16[32]{0:T(256)(128)(2,1)S(1)}, bf16[32]{0:T(256)(128)(2,1)}, u32[]{:S(2)}) copy-start(bf16[32]{0:T(256)(128)(2,1)} %param.6) | copy-start | bytes 196
  75.7 6.2 %copy-start.9 = (u32[128]{0:T(128)S(1)}, u32[128]{0:T(128)}, u32[]{:S(2)}) copy-start(u32[128]{0:T(128)} %constant.24) | copy-start | bytes 1540
  75.7 7.5 %copy-start.7 = (bf16[1,32,2048]{2,1,0:T(8,128)(2,1)S(1)}, bf16[1,32,2048]{2,1,0:T(8,128)(2,1)}, u32[]{:S(2)}) copy-start(bf16[1,32,2048]{2,1,0:T(8,128)(2,1)} %param.7) | copy-start | bytes 393220
  191.5 2.3 copy-start.1
Sparse Core Ops, SparseCore 0:
  62.5 124.4 all-reduce.4
  189.5 107.8 all-reduce.6
